TPU v7x, 32 devices: a whole 2x2x4 slice. The times are simulated.
32 devices in a mesh: rows: 16 (over z, y, x), cols: 2 (over core).
Axes of the slice: x: 2, y: 2, z: 4, core: 2. Of those that a mesh axis runs over, the one named last changes fastest.
Arguments:
- tokens_in: bfloat16 [6304, 768], P(('rows', 'cols')), may hold values from -6 to 6
- ln1_gain: float32 [768], replicated, may hold values from 0.5 to 1.5
- ln1_shift: float32 [768], replicated, may hold values from -4 to 4
- qkv_weight: bfloat16 [768, 2304], P(None, 'cols'), may hold values from -0.21875 to 0.21875
- out_weight: bfloat16 [768, 768], P('cols'), may hold values from -1.75 to 1.75
- ln2_gain: float32 [768], replicated, may hold values from 0.5 to 1.5
- ln2_shift: float32 [768], replicated, may hold values from -4 to 4
- router_weight: bfloat16 [768, 32], replicated, may hold values from -0.4375 to 0.4375
- expert_in: bfloat16 [768, 98304], P(None, ('rows', 'cols')), may hold values from -0.21875 to 0.21875
- expert_out: bfloat16 [98304, 768], P(('rows', 'cols')), may hold values from -0.4375 to 0.4375
- routes: int32 [6304, 2], P(('rows', 'cols')), may hold values from 0 to 31, all different within a row; in each aligned block of 197 rows (0 to 196, 197 to 393, ...) at most 16 rows name the same one
- cotangent: bfloat16 [6304, 768], P(('rows', 'cols')), may hold values from -6 to 6
Outputs:
- output: bfloat16 [6304, 768], P(('rows', 'cols'))
- tokens_grad: bfloat16 [6304, 768], P(('rows', 'cols'))
- ln1_gain_grad: float32 [768], replicated
- ln1_shift_grad: float32 [768], replicated
- qkv_grad: float32 [768, 2304], P(None, 'cols')
- out_grad: float32 [768, 768], P('cols')
- ln2_gain_grad: float32 [768], replicated
- ln2_shift_grad: float32 [768], replicated
- router_grad: float32 [768, 32], replicated
- expert_in_grad: float32 [768, 98304], P(None, ('rows', 'cols'))
- expert_out_grad: float32 [98304, 768], P(('rows', 'cols'))
Inputs may be any that keep to these rules, and one draw needn't show every extreme that they name: `routes`: the two experts of a token differ. Among the tokens of one device (aligned blocks of 197 rows) each expert is named by at most 16 assignments, a bound that some block reaches.
All inputs are finite; a program needn't handle non-finite values.
Results may differ from a plain program's by a relative error of at most 0.022.
Values may be sent and summed in bfloat16 or wider, within the bound.
A program may use at most 192 MiB of HBM per device.

v0:
```python
import jax
import jax.numpy as jnp
from jax import lax
from jax.sharding import PartitionSpec as P

DH = 64
FF = 3072
SEQ = 197
EPSILON = 1e-06


def layer_norm(values, norm_gain, norm_shift):
    average = jnp.mean(values, axis=-1, keepdims=True)
    centred = values - average
    variance = jnp.mean(centred * centred, axis=-1, keepdims=True)
    return centred * lax.rsqrt(variance + EPSILON) * norm_gain + norm_shift


def gelu_slope(pre_act):
    normal_cdf = 0.5 * (1.0 + jax.scipy.special.erf(pre_act * 0.7071067811865476))
    density = jnp.exp(-0.5 * pre_act * pre_act) * 0.3989422804014327
    return normal_cdf + pre_act * density


def dot_rows(first_side, second_side):
    return lax.dot_general(
        first_side, second_side, (((0,), (0,)), ((), ())), preferred_element_type=jnp.float32
    )


def dot_last(first_side, second_side):
    return lax.dot_general(
        first_side, second_side, (((1,), (1,)), ((), ())), preferred_element_type=jnp.float32
    )


def attention_scores(queries, keys_all, score_scale):
    scores = jnp.einsum("nqhd,nkhd->nhqk", queries, keys_all, preferred_element_type=jnp.float32)
    return scores * score_scale


def body(
    tokens_in,
    ln1_gain,
    ln1_shift,
    qkv_weight,
    out_weight,
    ln2_gain,
    ln2_shift,
    router_weight,
    expert_in,
    expert_out,
    routes,
    cotangent,
):
    local_rows = tokens_in.shape[0]
    model_width = tokens_in.shape[1]
    experts = router_weight.shape[1]
    capacity = max(2, 8 * local_rows // (3 * experts))
    heads_local = qkv_weight.shape[1] // (3 * DH)
    score_scale = DH ** (-0.5)
    row_count = lax.axis_size("rows")
    row_place = lax.axis_index("rows")
    col_place = lax.axis_index("cols")
    per_device = max(1, experts // row_count)
    copies = max(1, row_count // experts)
    slots = per_device * capacity
    piece_half = expert_in.shape[1]
    piece_whole = piece_half * lax.axis_size("cols")
    arrived_rows = row_count * slots
    tokens_f = tokens_in.astype(jnp.float32)
    normed_low = layer_norm(tokens_f, ln1_gain, ln1_shift).astype(jnp.bfloat16)
    gathered = lax.all_gather(normed_low, "cols", axis=0, tiled=True)
    pair_rows = gathered.shape[0]
    images = pair_rows // SEQ
    qkv_low = jnp.dot(gathered, qkv_weight, preferred_element_type=jnp.float32).astype(jnp.bfloat16)
    head_split = qkv_low.reshape(images, SEQ, heads_local, 3, DH)
    queries = head_split[:, :, :, 0]
    keys_all = head_split[:, :, :, 1]
    values_all = head_split[:, :, :, 2]
    scores = attention_scores(queries, keys_all, score_scale)
    score_peak = jnp.max(scores, axis=-1, keepdims=True)
    log_total = score_peak + jnp.log(jnp.sum(jnp.exp(scores - score_peak), axis=-1, keepdims=True))
    weights_low = jnp.exp(scores - log_total).astype(jnp.bfloat16)
    context = jnp.einsum(
        "nhqk,nkhd->nqhd", weights_low, values_all, preferred_element_type=jnp.float32
    )
    context_low = context.astype(jnp.bfloat16).reshape(pair_rows, heads_local * DH)
    row_block = context_low
    attn_out = lax.psum_scatter(
        jnp.dot(row_block, out_weight, preferred_element_type=jnp.float32),
        "cols",
        scatter_dimension=0,
        tiled=True,
    )
    hidden_one = tokens_f + attn_out
    mixed_low = layer_norm(hidden_one, ln2_gain, ln2_shift).astype(jnp.bfloat16)
    logits = jnp.dot(mixed_low, router_weight, preferred_element_type=jnp.float32)
    router_probs = jax.nn.softmax(logits, axis=-1)
    expert_ids = jnp.arange(experts, dtype=jnp.int32)
    chosen = (routes[:, :, None] == expert_ids[None, None, :]).astype(jnp.float32)
    gate_values = jnp.sum(router_probs[:, None, :] * chosen, axis=-1)
    flat_ids = routes.reshape(-1)
    flat_hot = (flat_ids[:, None] == expert_ids[None, :]).astype(jnp.int32)
    slot_ranks = jnp.sum(jnp.cumsum(flat_hot, axis=0) * flat_hot, axis=1) - 1
    first_device = flat_ids // per_device * copies
    slot_index = flat_ids % per_device * capacity + slot_ranks
    copy_ids = jnp.arange(copies, dtype=jnp.int32)
    targets = ((first_device[:, None] + copy_ids[None, :]) * slots + slot_index[:, None]).reshape(
        -1
    )
    grad_out = cotangent.astype(jnp.float32)
    grad_slots = (
        (gate_values[:, :, None] * grad_out[:, None, :])
        .astype(jnp.bfloat16)
        .reshape(2 * local_rows, model_width)
    )
    rows_send = (
        jnp.zeros((arrived_rows, model_width), jnp.bfloat16)
        .at[targets]
        .set(jnp.repeat(mixed_low, 2 * copies, axis=0))
    )
    grads_send = (
        jnp.zeros((arrived_rows, model_width), jnp.bfloat16)
        .at[targets]
        .set(jnp.repeat(grad_slots, copies, axis=0))
    )
    arrived, grad_result = (
        lax.all_to_all(
            rows_send.reshape(row_count, slots, model_width),
            "rows",
            split_axis=0,
            concat_axis=0,
            tiled=True,
        ),
        lax.all_to_all(
            grads_send.reshape(row_count, slots, model_width),
            "rows",
            split_axis=0,
            concat_axis=0,
            tiled=True,
        ),
    )
    arrived = arrived.reshape(arrived_rows, model_width)
    grad_result = grad_result.reshape(arrived_rows, model_width)
    unit_base = row_place % copies * piece_whole
    both_rows, both_grads = (
        lax.all_gather(arrived, "cols", axis=0, tiled=True),
        lax.all_gather(grad_result, "cols", axis=0, tiled=True),
    )
    slot_local = jnp.arange(both_rows.shape[0], dtype=jnp.int32) % slots // capacity
    unit_local = (
        unit_base + col_place * piece_half + jnp.arange(piece_half, dtype=jnp.int32)
    ) // FF
    mask = (slot_local[:, None] == unit_local[None, :]).astype(jnp.float32)
    pre_act = jnp.dot(both_rows, expert_in, preferred_element_type=jnp.float32) * mask
    act_low = jax.nn.gelu(pre_act, approximate=False).astype(jnp.bfloat16)
    result_low = lax.psum_scatter(
        jnp.dot(act_low, expert_out, preferred_element_type=jnp.float32).astype(jnp.bfloat16),
        "cols",
        scatter_dimension=0,
        tiled=True,
    )
    grad_act = dot_last(both_grads, expert_out)
    grad_pre_low = (grad_act * gelu_slope(pre_act) * mask).astype(jnp.bfloat16)
    first_grad = dot_rows(both_rows, grad_pre_low)
    second_grad = dot_rows(act_low, both_grads)
    grad_arrived = lax.psum_scatter(
        dot_last(grad_pre_low, expert_in).astype(jnp.bfloat16),
        "cols",
        scatter_dimension=0,
        tiled=True,
    )
    returned = lax.all_to_all(
        result_low.reshape(row_count, slots, model_width),
        "rows",
        split_axis=0,
        concat_axis=0,
        tiled=True,
    )
    returned = returned.reshape(arrived_rows, model_width)
    picked = jnp.sum(
        returned[targets].reshape(local_rows, 2, copies, model_width).astype(jnp.float32), axis=2
    )
    output = (hidden_one + jnp.sum(gate_values[:, :, None] * picked, axis=1)).astype(jnp.bfloat16)
    grad_gates = jnp.sum(grad_out[:, None, :] * picked, axis=-1)
    grad_sent = lax.all_to_all(
        grad_arrived.reshape(row_count, slots, model_width),
        "rows",
        split_axis=0,
        concat_axis=0,
        tiled=True,
    )
    grad_sent = grad_sent.reshape(arrived_rows, model_width)
    grad_mixed_experts = jnp.sum(
        grad_sent[targets].reshape(local_rows, 2 * copies, model_width).astype(jnp.float32), axis=1
    )
    gate_term = jnp.sum(grad_gates * gate_values, axis=-1, keepdims=True)
    grad_probs = jnp.sum(chosen * grad_gates[:, :, None], axis=1)
    grad_logits_low = (router_probs * (grad_probs - gate_term)).astype(jnp.bfloat16)
    router_grad = dot_rows(mixed_low, grad_logits_low)
    grad_mixed = dot_last(grad_logits_low, router_weight) + grad_mixed_experts
    unused_two, norm_two_back = jax.vjp(layer_norm, hidden_one, ln2_gain, ln2_shift)
    grad_hidden_part, ln2_gain_grad, ln2_shift_grad = norm_two_back(grad_mixed)
    grad_hidden = grad_out + grad_hidden_part
    grad_attn_low = grad_hidden.astype(jnp.bfloat16)
    grad_attn_all = lax.all_gather(grad_attn_low, "cols", axis=0, tiled=True)
    out_grad = dot_rows(context_low, grad_attn_all)
    grad_context = (
        dot_last(grad_attn_all, out_weight)
        .astype(jnp.bfloat16)
        .reshape(images, SEQ, heads_local, DH)
    )
    scores_again = attention_scores(queries, keys_all, score_scale)
    attn_probs = jnp.exp(scores_again - log_total)
    probs_low = attn_probs.astype(jnp.bfloat16)
    grad_values = jnp.einsum(
        "nhqk,nqhd->nkhd", probs_low, grad_context, preferred_element_type=jnp.float32
    )
    grad_weights = jnp.einsum(
        "nqhd,nkhd->nhqk", grad_context, values_all, preferred_element_type=jnp.float32
    )
    row_term = jnp.sum(grad_weights * attn_probs, axis=-1, keepdims=True)
    grad_scores = (attn_probs * (grad_weights - row_term)).astype(jnp.bfloat16)
    grad_queries = (
        jnp.einsum("nhqk,nkhd->nqhd", grad_scores, keys_all, preferred_element_type=jnp.float32)
        * score_scale
    )
    grad_keys = (
        jnp.einsum("nhqk,nqhd->nkhd", grad_scores, queries, preferred_element_type=jnp.float32)
        * score_scale
    )
    grad_qkv = (
        jnp.stack([grad_queries, grad_keys, grad_values], axis=3)
        .astype(jnp.bfloat16)
        .reshape(pair_rows, 3 * heads_local * DH)
    )
    qkv_grad = dot_rows(gathered, grad_qkv)
    row_block = grad_qkv
    grad_normed = lax.psum_scatter(
        dot_last(row_block, qkv_weight).astype(jnp.bfloat16),
        "cols",
        scatter_dimension=0,
        tiled=True,
    ).astype(jnp.float32)
    unused_one, norm_one_back = jax.vjp(layer_norm, tokens_f, ln1_gain, ln1_shift)
    grad_tokens_part, ln1_gain_grad, ln1_shift_grad = norm_one_back(grad_normed)
    tokens_grad = (grad_hidden + grad_tokens_part).astype(jnp.bfloat16)
    qkv_grad, out_grad = lax.psum((qkv_grad, out_grad), "rows")
    router_grad, ln1_gain_grad, ln1_shift_grad, ln2_gain_grad, ln2_shift_grad = lax.psum(
        (router_grad, ln1_gain_grad, ln1_shift_grad, ln2_gain_grad, ln2_shift_grad),
        ("rows", "cols"),
    )
    return (
        output,
        tokens_grad,
        ln1_gain_grad,
        ln1_shift_grad,
        qkv_grad,
        out_grad,
        ln2_gain_grad,
        ln2_shift_grad,
        router_grad,
        first_grad,
        second_grad,
    )


def solution(mesh):
    in_specs = (
        P(("rows", "cols"), None),
        P(),
        P(),
        P(None, "cols"),
        P("cols", None),
        P(),
        P(),
        P(),
        P(None, ("rows", "cols")),
        P(("rows", "cols"), None),
        P(("rows", "cols"), None),
        P(("rows", "cols"), None),
    )
    out_specs = (
        P(("rows", "cols"), None),
        P(("rows", "cols"), None),
        P(),
        P(),
        P(None, "cols"),
        P("cols", None),
        P(),
        P(),
        P(),
        P(None, ("rows", "cols")),
        P(("rows", "cols"), None),
    )
    return jax.shard_map(body, mesh=mesh, in_specs=in_specs, out_specs=out_specs, check_vma=False)
```

profile of v0, /device:TPU:0, one launch (start us, length us, event | category | flops | bytes accessed | tf_op | source)
XLA Modules:
  0.0 595.0 jit_solution(453533763309978735)
XLA Ops:
  17.7 7.0 %fusion.72 = (bf16[2,197,6,1,64]{4,3,2,1,0:T(2,128)(2,1)S(1)}, bf16[2,197,6,1,64]{4,3,2,1,0:T(2,128)(2,1)}, bf16[2,197,6,1,64]{4,3,2,1,0:T(2,128)(2,1)}) fusion(bf16[2,197,6,3,64]{4,3,2,1,0:T(4,128)(2,1)} %reshape.405), kind=kLoop, calls=%fused_computation.161 | loop fusion | bytes 1815552 | tf_op jit(solution)/shard_map/slice | solution.py:78
  39.8 4.9 fusion
  56.2 3.9 scatter_custom_fusion
  60.0 8.3 %all-to-all-start = ((bf16[16,32,768]{2,1,0:T(8,128)(2,1)}), bf16[16,32,768]{2,1,0:T(8,128)(2,1)}, u32[]{:S(2)}, u32[]{:S(2)}) async-start(bf16[16,32,768]{2,1,0:T(8,128)(2,1)} %bitcast.8), calls=%async_computation | async-start | bytes 1572864 | tf_op jit(solution)/shard_map/all_to_all | solution.py:129
  72.2 15.5 %all-to-all-done = bf16[16,32,768]{2,1,0:T(8,128)(2,1)} async-done(((bf16[16,32,768]{2,1,0:T(8,128)(2,1)}), bf16[16,32,768]{2,1,0:T(8,128)(2,1)}, u32[]{:S(2)}, u32[]{:S(2)}) %all-to-all-start) | async-done | bytes 786464 | tf_op jit(solution)/shard_map/all_to_all | solution.py:129
  91.2 4.9 all-to-all-start.2
  96.2 18.6 %all-to-all-done.2 = bf16[16,32,768]{2,1,0:T(8,128)(2,1)S(1)} async-done(((bf16[16,32,768]{2,1,0:T(8,128)(2,1)}), bf16[16,32,768]{2,1,0:T(8,128)(2,1)S(1)}, u32[]{:S(2)}, u32[]{:S(2)}) %all-to-all-start.2) | async-done | bytes 786464 | tf_op jit(solution)/shard_map/all_to_all | solution.py:136
  115.8 35.3 %fusion.5 = (bf16[1024,3072]{1,0:T(8,128)(2,1)S(1)}, f32[1024,3072]{1,0:T(8,128)}) fusion(s32[3072]{0:T(1024)S(1)} %add_select_fusion, s32[1024]{0:T(1024)S(1)} %add_select_fusion.1, bf16[1024,768]{1,0:T(8,128)(2,1)} %all-gather.5.cloned.1.call-done, bf16[768,3072]{1,0:T(8,128)(2,1)} %param.20), kind=kOutput, calls=%fused_computation.11 | convolution fusion | flops 5042601984 | bytes 25182208 | tf_op jit(solution)/shard_map/dot_general | solution.py:156
  153.8 8.5 %convolution_convert_fusion.2 = bf16[1024,768]{1,0:T(8,128)(2,1)} fusion(bf16[1024,3072]{1,0:T(8,128)(2,1)S(1)} %get-tuple-element.37, bf16[3072,768]{1,0:T(8,128)(2,1)} %param.21), kind=kOutput, calls=%fused_computation.39 | convolution fusion | flops 4832624640 | bytes 12582912 | tf_op jit(solution)/shard_map/dot_general | solution.py:159
  162.3 8.7 %reduce-scatter.9.cloned.1.call-start = ((), (), s32[]{:S(2)}) async-start(), calls=%async_computation.9 | async-start | bytes 2359296 | tf_op jit(solution)/shard_map/reduce_scatter | solution.py:168
  171.1 12.0 %fusion.2 = bf16[1024,3072]{1,0:T(8,128)(2,1)S(1)} fusion(f32[1024,3072]{1,0:T(8,128)} %get-tuple-element.38, bf16[1024,768]{1,0:T(8,128)(2,1)} %all-gather.7.cloned.1.call-done, bf16[3072,768]{1,0:T(8,128)(2,1)} %param.21, s32[3072]{0:T(1024)S(1)} %add_select_fusion, s32[1024]{0:T(1024)S(1)} %add_select_fusion.1), kind=kOutput, calls=%fused_computation.8 | convolution fusion | flops 4872732672 | bytes 25182208 | tf_op jit(solution)/shard_map/dot_general | solution.py:32
  185.8 6.3 %convolution_convert_fusion.1 = bf16[1024,768]{1,0:T(8,128)(2,1)} fusion(bf16[1024,3072]{1,0:T(8,128)(2,1)S(1)} %fusion.2, bf16[768,3072]{1,0:T(8,128)(2,1)S(1)} %bitcast.115), kind=kOutput, calls=%fused_computation.38 | convolution fusion | flops 4832624640 | bytes 12582912 | tf_op jit(solution)/shard_map/dot_general | solution.py:32
  192.1 5.2 all-to-all-start.1
  200.8 15.2 %all-to-all-done.1 = bf16[16,32,768]{2,1,0:T(8,128)(2,1)S(1)} async-done(((bf16[16,32,768]{2,1,0:T(8,128)(2,1)}), bf16[16,32,768]{2,1,0:T(8,128)(2,1)S(1)}, u32[]{:S(2)}, u32[]{:S(2)}) %all-to-all-start.1) | async-done | bytes 786464 | tf_op jit(solution)/shard_map/all_to_all | solution.py:174
  216.0 4.9 all-to-all-start.3
  228.2 4.7 multiply_reduce_fusion.2
  234.1 5.3 all-to-all-done.3
  270.2 4.6 fusion.75
  276.4 10.0 %fusion.79 = f32[3072,768]{1,0:T(8,128)} fusion(bf16[1024,3072]{1,0:T(8,128)(2,1)} %copy-done.44, bf16[1024,768]{1,0:T(8,128)(2,1)} %all-gather.7.cloned.1.call-done), kind=kOutput, calls=%fused_computation.168 | convolution fusion | flops 4831838208 | bytes 17301504 | tf_op jit(solution)/shard_map/dot_general | solution.py:26
  294.5 9.9 %fusion.78 = f32[768,3072]{1,0:T(8,128)} fusion(bf16[1024,768]{1,0:T(8,128)(2,1)} %all-gather.5.cloned.1.call-done, bf16[1024,3072]{1,0:T(8,128)(2,1)} %copy-done.43), kind=kOutput, calls=%fused_computation.167 | convolution fusion | flops 4831838208 | bytes 17301504 | tf_op jit(solution)/shard_map/dot_general | solution.py:26
  307.3 40.2 %all-reduce.5 = (f32[768]{0:T(1024)}, f32[768]{0:T(1024)}, f32[768]{0:T(1024)}, f32[768]{0:T(1024)}) all-reduce(f32[768]{0:T(1024)S(1)} %get-tuple-element.15, f32[768]{0:T(1024)S(1)} %get-tuple-element.18, f32[768]{0:T(1024)S(1)} %get-tuple-element.11, ...), channel_id=1, replica_groups=mesh['rows'=16,'cols'=2] {'rows','cols'}, use_global_device_ids=true, to_apply=%region_29.30 | all-reduce | flops 3072 | bytes 24576 | tf_op jit(solution)/shard_map/psum | solution.py:250
  348.6 46.3 %all-reduce.10.cloned.1.call-done = f32[768,32]{0,1:T(8,128)} async-done(((f32[768,32]{0,1:T(8,128)}), f32[768,32]{0,1:T(8,128)}) %all-reduce.10.cloned.1.call-update) | async-done | bytes 98320 | tf_op jit(solution)/shard_map/psum | solution.py:250
  394.8 187.2 %all-reduce.12.cloned.1.call-done = (f32[768,1152]{1,0:T(8,128)}, f32[384,768]{1,0:T(8,128)}) async-done(((f32[768,1152]{1,0:T(8,128)}, f32[384,768]{1,0:T(8,128)}), (f32[768,1152]{1,0:T(8,128)}, f32[384,768]{1,0:T(8,128)})) %all-reduce.12.cloned.1.call-update) | async-done | bytes 4718608 | tf_op jit(solution)/shard_map/psum | solution.py:249
  582.0 4.1 copy.130
  (209 shorter events, 107.7 us)
Async XLA Ops:
  36.0 16.9 %copy-start.5 = (bf16[197,768]{1,0:T(8,128)(2,1)S(1)}, bf16[197,768]{1,0:T(8,128)(2,1)}, u32[]{:S(2)}) copy-start(bf16[197,768]{1,0:T(8,128)(2,1)} %param.12) | copy-start | bytes 907780
  37.1 16.9 %copy-start.28 = (f32[768]{0:T(1024)S(1)}, f32[768]{0:T(1024)}, u32[]{:S(2)}) copy-start(f32[768]{0:T(1024)} %param.17) | copy-start | bytes 9220
  37.1 16.9 %copy-start.41 = (f32[768]{0:T(1024)S(1)}, f32[768]{0:T(1024)}, u32[]{:S(2)}) copy-start(f32[768]{0:T(1024)} %param.18) | copy-start | bytes 9220
  45.4 5.4 collective-permute-start
  47.9 20.5 %copy-start.9 = (bf16[197,768]{1,0:T(8,128)(2,1)S(1)}, bf16[197,768]{1,0:T(8,128)(2,1)}, u32[]{:S(2)}) copy-start(bf16[197,768]{1,0:T(8,128)(2,1)} %param.23) | copy-start | bytes 907780
  53.4 18.8 %copy-start.39 = (f32[197]{0:T(256)}, f32[197]{0:T(256)S(1)}, u32[]{:S(2)}) copy-start(f32[197]{0:T(256)S(1)} %multiply_reduce_fusion.6) | copy-start | bytes 2368
  53.4 18.5 %copy-start.25 = (bf16[768,32]{0,1:T(8,128)(2,1)S(1)}, bf16[768,32]{0,1:T(8,128)(2,1)}, u32[]{:S(2)}) copy-start(bf16[768,32]{0,1:T(8,128)(2,1)} %param.19) | copy-start | bytes 147460
  53.9 18.2 %copy-start.34 = (f32[197]{0:T(256)}, f32[197]{0:T(256)S(1)}, u32[]{:S(2)}) copy-start(f32[197]{0:T(256)S(1)} %fusion.67) | copy-start | bytes 2368
  54.1 33.6 %copy-start.11 = (bf16[197,768]{1,0:T(8,128)(2,1)}, bf16[197,768]{1,0:T(8,128)(2,1)S(1)}, u32[]{:S(2)}) copy-start(bf16[197,768]{1,0:T(8,128)(2,1)S(1)} %add_convert_fusion.2) | copy-start | bytes 907780
  60.0 27.7 %all-to-all-start = ((bf16[16,32,768]{2,1,0:T(8,128)(2,1)}), bf16[16,32,768]{2,1,0:T(8,128)(2,1)}, u32[]{:S(2)}, u32[]{:S(2)}) async-start(bf16[16,32,768]{2,1,0:T(8,128)(2,1)} %bitcast.8), calls=%async_computation | async-start | bytes 1572864 | tf_op jit(solution)/shard_map/all_to_all | solution.py:129
  68.3 47.4 %all-gather.5.cloned.1.call-start = ((), (), s32[]{:S(2)}) async-start(), calls=%async_computation.6 | async-start | bytes 2359296 | tf_op jit(solution)/shard_map/all_gather | solution.py:148
  72.2 15.5 %copy-start.36 = (f32[197]{0:T(256)}, f32[197]{0:T(256)S(1)}, u32[]{:S(2)}) copy-start(f32[197]{0:T(256)S(1)} %fusion.55) | copy-start | bytes 2368
  91.2 23.5 %all-to-all-start.2 = ((bf16[16,32,768]{2,1,0:T(8,128)(2,1)}), bf16[16,32,768]{2,1,0:T(8,128)(2,1)S(1)}, u32[]{:S(2)}, u32[]{:S(2)}) async-start(bf16[16,32,768]{2,1,0:T(8,128)(2,1)} %bitcast.107), calls=%async_computation.3 | async-start | bytes 1572864 | tf_op jit(solution)/shard_map/all_to_all | solution.py:136
  96.1 74.9 %all-gather.7.cloned.1.call-start = ((), (), s32[]{:S(2)}) async-start(), calls=%async_computation.8 | async-start | bytes 2359296 | tf_op jit(solution)/shard_map/all_gather | solution.py:149
  115.7 76.4 %reduce-scatter.7.cloned.1.call-start = ((), (), s32[]{:S(2)}) async-start(), calls=%async_computation.7 | async-start | bytes 2359296 | tf_op jit(solution)/shard_map/reduce_scatter | solution.py:158
  153.8 32.0 %slice-start = ((s8[4718592]{0:T(1024)(128)(4,1)}), s8[524288]{0:T(1024)(128)(4,1)S(1)}, s32[]{:S(2)}) async-start(s8[4718592]{0:T(1024)(128)(4,1)} %bitcast.114), calls=%async_computation.12 | async-start | bytes 1048576
  162.3 38.5 %reduce-scatter.9.cloned.1.call-start = ((), (), s32[]{:S(2)}) async-start(), calls=%async_computation.9 | async-start | bytes 2359296 | tf_op jit(solution)/shard_map/reduce_scatter | solution.py:168
  192.1 23.9 %all-to-all-start.1 = ((bf16[16,32,768]{2,1,0:T(8,128)(2,1)}), bf16[16,32,768]{2,1,0:T(8,128)(2,1)S(1)}, u32[]{:S(2)}, u32[]{:S(2)}) async-start(bf16[16,32,768]{2,1,0:T(8,128)(2,1)} %bitcast.109), calls=%async_computation.2 | async-start | bytes 1572864 | tf_op jit(solution)/shard_map/all_to_all | solution.py:174
  216.0 23.5 %all-to-all-start.3 = ((bf16[16,32,768]{2,1,0:T(8,128)(2,1)}), bf16[16,32,768]{2,1,0:T(8,128)(2,1)S(1)}, u32[]{:S(2)}, u32[]{:S(2)}) async-start(bf16[16,32,768]{2,1,0:T(8,128)(2,1)} %bitcast.108), calls=%async_computation.5 | async-start | bytes 1572864 | tf_op jit(solution)/shard_map/all_to_all | solution.py:187
  220.9 174.0 %all-reduce.10.cloned.1.call-start = ((), (), s32[]{:S(2)}) async-start(), calls=%async_computation.10 | async-start | bytes 196608 | tf_op jit(solution)/shard_map/psum | solution.py:250
  232.8 15.6 %copy-start.4 = (f32[197,768]{1,0:T(8,128)S(1)}, f32[197,768]{1,0:T(8,128)}, u32[]{:S(2)}) copy-start(f32[197,768]{1,0:T(8,128)} %copy-done.3) | copy-start | bytes 1815556
  274.9 307.1 %all-reduce.12.cloned.1.call-start = ((), (), s32[]{:S(2)}) async-start(), calls=%async_computation.11 | async-start | bytes 9437184 | tf_op jit(solution)/shard_map/psum | solution.py:249
  291.8 55.6 %copy-start.8 = (f32[197,768]{1,0:T(8,128)S(1)}, f32[197,768]{1,0:T(8,128)}, u32[]{:S(2)}) copy-start(f32[197,768]{1,0:T(8,128)} %copy-done.7) | copy-start | bytes 1815556
  291.8 12.5 %collective-permute-start.1 = (bf16[3,768]{1,0:T(4,128)(2,1)S(1)}, bf16[3,768]{1,0:T(4,128)(2,1)S(1)}, u32[]{:S(2)}, u32[]{:S(2)}) collective-permute-start(bf16[3,768]{1,0:T(4,128)(2,1)S(1)} %slice.34), channel_id=1, source_target_pairs={{0,1},{2,3},{4,5},{6,7},{8,9},{10,11},{12,13},{14,15},{16,17},{18,... | collective-permute-start | bytes 13832
  (35 other events, 221.9 us)
Sparse Core Ops, SparseCore 0:
  87.9 9.0 all-gather.4
  115.8 9.0 all-gather.6
  162.4 8.3 reduce-scatter.6
  192.2 8.5 reduce-scatter.8
  275.0 119.7 all-reduce.9
  401.0 180.9 all-reduce.11
where the time goes:
time: 605 us; the launch traced here: 595 us
  waiting for transfers between devices  292 us (48%)
  matrix products  103 us (17%)
  local copies, waits for them, and re-layouts  68.5 us (11%)
  blocking collectives  53.4 us (9%)
  starting transfers between devices  36.9 us (6%)
  other arithmetic  25.5 us (4%)
  between operations  16.1 us (3%)
    psum x1, waiting for transfers between devices, body(): qkv_grad, out_grad = lax.psum((qkv_grad, out_grad), 'rows')  187 us
    psum x1, waiting for transfers between devices, body(): lax.psum((router_grad, ln1_gain_grad, ln1_shift_grad, ln2_gain_grad, ln2_...  46.3 us
    psum x1, blocking collectives, body(): lax.psum((router_grad, ln1_gain_grad, ln1_shift_grad, ln2_gain_grad, ln2_...  40.2 us
    dot_general x1, matrix products, body(): jnp.dot(both_rows, expert_in, preferred_element_type=jnp.float32) * mask  35.3 us
    unnamed x108, local copies, waits for them, and re-layouts  30.5 us
    dot_general x5, matrix products, dot_rows(): lax.dot_general(first_side, second_side, (((0,), (0,)), ((), ())), prefer...  26.8 us
    dot_general x5, matrix products, dot_last(): lax.dot_general(first_side, second_side, (((1,), (1,)), ((), ())), prefer...  22.5 us
    all_to_all x1, waiting for transfers between devices, body(): lax.all_to_all(grads_send.reshape(row_count, slots, model_width), 'rows',...  18.6 us
  transfers between devices with their start and end apart: 12, of which 7 were waited for; matrix products, arithmetic and copies ran while one was open for 19% of the time, Pallas kernels for 0%

commit v1 on v0

--- a/solution.py
+++ b/solution.py
@@ -7,6 +7,30 @@
 FF = 3072
 SEQ = 197
 EPSILON = 1e-06
+
+
+def cut_along(value, dim, peers):
+    shape = value.shape
+    tiles = value.reshape(*shape[:dim], peers, shape[dim] // peers, *shape[dim + 1 :])
+    return jnp.moveaxis(tiles, dim, 0)
+
+
+def joined_along(pieces, dim):
+    pieces = jnp.moveaxis(pieces, 0, dim)
+    lengths = pieces.shape
+    return pieces.reshape(*lengths[:dim], lengths[dim] * lengths[dim + 1], *lengths[dim + 2 :])
+
+
+def exchange_directly(shard, axis, split_dim, concat_dim):
+    size, position = (lax.axis_size(axis), lax.axis_index(axis))
+    blocks = cut_along(shard, split_dim, size)
+    out = blocks
+    for turn in range(1, size):
+        target, source = ((position + turn) % size, (position - turn) % size)
+        sent = lax.dynamic_index_in_dim(blocks, target, 0)
+        other = lax.ppermute(sent, axis, [(i, (i + turn) % size) for i in range(size)])
+        out = lax.dynamic_update_slice_in_dim(out, other, source, axis=0)
+    return joined_along(out, concat_dim)
 
 
 def layer_norm(values, norm_gain, norm_shift):
@@ -126,13 +150,7 @@
         .set(jnp.repeat(grad_slots, copies, axis=0))
     )
     arrived, grad_result = (
-        lax.all_to_all(
-            rows_send.reshape(row_count, slots, model_width),
-            "rows",
-            split_axis=0,
-            concat_axis=0,
-            tiled=True,
-        ),
+        exchange_directly(rows_send.reshape(row_count, slots, model_width), "rows", 0, 0),
         lax.all_to_all(
             grads_send.reshape(row_count, slots, model_width),
             "rows",

time: 605 us -> 565 us (0.934)
  waiting for transfers between devices: 292 us -> 241 us
  starting transfers between devices: 36.9 us -> 48.6 us
    psum x1, waiting for transfers between devices: 46.3 us -> 10.9 us  [body(): lax.psum((router_grad, ln1_gain_grad, ln1_shift_grad, ln2_gain_grad, ln2_...]
    ppermute x0 -> x15, starting transfers between devices: none -> 26.6 us  [exchange_directly(): lax.ppermute(sent, axis, [(i, (i + turn) % size) for i in range(size)])]
    all_to_all x1 -> x0, waiting for transfers between devices: 15.5 us -> none  [body(): lax.all_to_all(rows_send.reshape(row_count, slots, model_width), 'rows',...]
    reduce_scatter x1, starting transfers between devices: 8.75 us -> 0.45 us  [body(): lax.psum_scatter(dot_last(grad_pre_low, expert_in).astype(jnp.bfloat16),...]
    all_to_all x1 -> x0, starting transfers between devices: 8.28 us -> none  [body(): lax.all_to_all(rows_send.reshape(row_count, slots, model_width), 'rows',...]
    ppermute x0 -> x15, waiting for transfers between devices: none -> 7.07 us  [exchange_directly(): lax.ppermute(sent, axis, [(i, (i + turn) % size) for i in range(size)])]
    unnamed x108 -> x94, local copies, waits for them, and re-layouts: 30.5 us -> 29.8 us
  transfers between devices with their start and end apart: 12 -> 26, of which waited for: 7 -> 11; matrix products, arithmetic and copies ran while one was open for 19% -> 27% of each run, Pallas kernels for 0% -> 0%
where the time goes in v1:
time: 565 us; the launch traced here: 558 us
  waiting for transfers between devices  241 us (43%)
  matrix products  104 us (18%)
  local copies, waits for them, and re-layouts  67.5 us (12%)
  blocking collectives  53.1 us (9%)
  starting transfers between devices  48.6 us (9%)
  other arithmetic  26.7 us (5%)
  between operations  16.4 us (3%)
    psum x1, waiting for transfers between devices, body(): qkv_grad, out_grad = lax.psum((qkv_grad, out_grad), 'rows')  187 us
    psum x1, blocking collectives, body(): lax.psum((router_grad, ln1_gain_grad, ln1_shift_grad, ln2_gain_grad, ln2_...  39.6 us
    dot_general x1, matrix products, body(): jnp.dot(both_rows, expert_in, preferred_element_type=jnp.float32) * mask  35.3 us
    unnamed x94, local copies, waits for them, and re-layouts  29.8 us
    dot_general x5, matrix products, dot_rows(): lax.dot_general(first_side, second_side, (((0,), (0,)), ((), ())), prefer...  26.8 us
    ppermute x15, starting transfers between devices, exchange_directly(): lax.ppermute(sent, axis, [(i, (i + turn) % size) for i in range(size)])  26.6 us
    dot_general x5, matrix products, dot_last(): lax.dot_general(first_side, second_side, (((1,), (1,)), ((), ())), prefer...  22.6 us
    all_to_all x1, waiting for transfers between devices, body(): lax.all_to_all(grads_send.reshape(row_count, slots, model_width), 'rows',...  14.2 us
  transfers between devices with their start and end apart: 26, of which 11 were waited for; matrix products, arithmetic and copies ran while one was open for 27% of the time, Pallas kernels for 0%

profile of v1, /device:TPU:0, one launch (start us, length us, event | category | flops | bytes accessed | tf_op | source)
XLA Modules:
  0.0 557.8 jit_solution(12346881713360458730)
XLA Ops:
  17.8 7.0 %fusion.72 = (bf16[2,197,6,1,64]{4,3,2,1,0:T(2,128)(2,1)S(1)}, bf16[2,197,6,1,64]{4,3,2,1,0:T(2,128)(2,1)}, bf16[2,197,6,1,64]{4,3,2,1,0:T(2,128)(2,1)}) fusion(bf16[2,197,6,3,64]{4,3,2,1,0:T(4,128)(2,1)} %reshape.397), kind=kLoop, calls=%fused_computation.191 | loop fusion | bytes 1815552 | tf_op jit(solution)/shard_map/slice | solution.py:102
  27.3 3.7 copy.122
  41.9 5.2 fusion
  69.9 5.0 collective-permute-done
  102.1 3.9 scatter_custom_fusion.1
  106.1 7.2 %all-to-all-start.1 = ((bf16[16,32,768]{2,1,0:T(8,128)(2,1)}), bf16[16,32,768]{2,1,0:T(8,128)(2,1)S(1)}, u32[]{:S(2)}, u32[]{:S(2)}) async-start(bf16[16,32,768]{2,1,0:T(8,128)(2,1)} %bitcast.110), calls=%async_computation.2 | async-start | bytes 1572864 | tf_op jit(solution)/shard_map/all_to_all | solution.py:154
  113.4 14.2 %all-to-all-done.1 = bf16[16,32,768]{2,1,0:T(8,128)(2,1)S(1)} async-done(((bf16[16,32,768]{2,1,0:T(8,128)(2,1)}), bf16[16,32,768]{2,1,0:T(8,128)(2,1)S(1)}, u32[]{:S(2)}, u32[]{:S(2)}) %all-to-all-start.1) | async-done | bytes 786464 | tf_op jit(solution)/shard_map/all_to_all | solution.py:154
  128.8 35.3 %fusion.5 = (bf16[1024,3072]{1,0:T(8,128)(2,1)S(1)}, f32[1024,3072]{1,0:T(8,128)}) fusion(s32[3072]{0:T(1024)S(1)} %add_select_fusion, s32[1024]{0:T(1024)S(1)} %add_select_fusion.1, bf16[1024,768]{1,0:T(8,128)(2,1)} %all-gather.5.cloned.1.call-done, bf16[768,3072]{1,0:T(8,128)(2,1)} %param.20), kind=kOutput, calls=%fused_computation.11 | convolution fusion | flops 5042601984 | bytes 25182208 | tf_op jit(solution)/shard_map/dot_general | solution.py:174
  166.8 8.5 %convolution_convert_fusion.2 = bf16[1024,768]{1,0:T(8,128)(2,1)} fusion(bf16[1024,3072]{1,0:T(8,128)(2,1)S(1)} %get-tuple-element.52, bf16[3072,768]{1,0:T(8,128)(2,1)} %param.21), kind=kOutput, calls=%fused_computation.39 | convolution fusion | flops 4832624640 | bytes 12582912 | tf_op jit(solution)/shard_map/dot_general | solution.py:177
  175.8 12.1 %fusion.2 = bf16[1024,3072]{1,0:T(8,128)(2,1)S(1)} fusion(f32[1024,3072]{1,0:T(8,128)} %get-tuple-element.53, bf16[1024,768]{1,0:T(8,128)(2,1)} %all-gather.7.cloned.1.call-done, bf16[3072,768]{1,0:T(8,128)(2,1)} %param.21, s32[3072]{0:T(1024)S(1)} %add_select_fusion, s32[1024]{0:T(1024)S(1)} %add_select_fusion.1), kind=kOutput, calls=%fused_computation.8 | convolution fusion | flops 4872732672 | bytes 25182208 | tf_op jit(solution)/shard_map/dot_general | solution.py:56
  190.6 6.3 %convolution_convert_fusion.1 = bf16[1024,768]{1,0:T(8,128)(2,1)} fusion(bf16[1024,3072]{1,0:T(8,128)(2,1)S(1)} %fusion.2, bf16[768,3072]{1,0:T(8,128)(2,1)S(1)} %bitcast.118), kind=kOutput, calls=%fused_computation.38 | convolution fusion | flops 4832624640 | bytes 12582912 | tf_op jit(solution)/shard_map/dot_general | solution.py:56
  196.9 4.7 all-to-all-start
  201.7 3.6 reduce-scatter.9.cloned.1.call-done
  205.3 13.1 %all-to-all-done = bf16[16,32,768]{2,1,0:T(8,128)(2,1)S(1)} async-done(((bf16[16,32,768]{2,1,0:T(8,128)(2,1)}), bf16[16,32,768]{2,1,0:T(8,128)(2,1)S(1)}, u32[]{:S(2)}, u32[]{:S(2)}) %all-to-all-start) | async-done | bytes 786464 | tf_op jit(solution)/shard_map/all_to_all | solution.py:192
  218.3 4.4 all-to-all-start.2
  230.1 4.7 multiply_reduce_fusion.2
  235.8 5.0 all-to-all-done.2
  269.2 4.6 fusion.75
  275.3 10.0 %fusion.79 = f32[3072,768]{1,0:T(8,128)} fusion(bf16[1024,3072]{1,0:T(8,128)(2,1)} %copy-done.37, bf16[1024,768]{1,0:T(8,128)(2,1)} %all-gather.7.cloned.1.call-done), kind=kOutput, calls=%fused_computation.198 | convolution fusion | flops 4831838208 | bytes 17301504 | tf_op jit(solution)/shard_map/dot_general | solution.py:50
  293.4 9.9 %fusion.78 = f32[768,3072]{1,0:T(8,128)} fusion(bf16[1024,768]{1,0:T(8,128)(2,1)} %all-gather.5.cloned.1.call-done, bf16[1024,3072]{1,0:T(8,128)(2,1)} %copy-done.36), kind=kOutput, calls=%fused_computation.197 | convolution fusion | flops 4831838208 | bytes 17301504 | tf_op jit(solution)/shard_map/dot_general | solution.py:50
  306.1 39.6 %all-reduce.5 = (f32[768]{0:T(1024)}, f32[768]{0:T(1024)}, f32[768]{0:T(1024)}, f32[768]{0:T(1024)}) all-reduce(f32[768]{0:T(1024)S(1)} %get-tuple-element.15, f32[768]{0:T(1024)S(1)} %get-tuple-element.18, f32[768]{0:T(1024)S(1)} %get-tuple-element.11, ...), channel_id=1, replica_groups=mesh['rows'=16,'cols'=2] {'rows','cols'}, use_global_device_ids=true, to_apply=%region_29.30 | all-reduce | flops 3072 | bytes 24576 | tf_op jit(solution)/shard_map/psum | solution.py:268
  346.9 10.9 %all-reduce.10.cloned.1.call-done = f32[768,32]{0,1:T(8,128)} async-done(((f32[768,32]{0,1:T(8,128)}), f32[768,32]{0,1:T(8,128)}) %all-reduce.10.cloned.1.call-update) | async-done | bytes 98320 | tf_op jit(solution)/shard_map/psum | solution.py:268
  357.8 187.2 %all-reduce.12.cloned.1.call-done = (f32[768,1152]{1,0:T(8,128)}, f32[384,768]{1,0:T(8,128)}) async-done(((f32[768,1152]{1,0:T(8,128)}, f32[384,768]{1,0:T(8,128)}), (f32[768,1152]{1,0:T(8,128)}, f32[384,768]{1,0:T(8,128)})) %all-reduce.12.cloned.1.call-update) | async-done | bytes 4718608 | tf_op jit(solution)/shard_map/psum | solution.py:267
  544.9 4.1 copy.145
  (239 shorter events, 131.2 us)
Async XLA Ops:
  7.2 121.6 %all-gather.5.cloned.1.call-start = ((), (), s32[]{:S(2)}) async-start(), calls=%async_computation.5 | async-start | bytes 2359296 | tf_op jit(solution)/shard_map/all_gather | solution.py:166
  47.1 12.7 %collective-permute-start.15 = (f32[3,768]{1,0:T(4,128)S(1)}, f32[3,768]{1,0:T(4,128)S(1)}, u32[]{:S(2)}, u32[]{:S(2)}) collective-permute-start(f32[3,768]{1,0:T(4,128)S(1)} %slice.33), channel_id=1, source_target_pairs={{0,1},{2,3},{4,5},{6,7},{8,9},{10,11},{12,13},{14,15},{16,17},{18,... | collective-permute-start | bytes 27656
  65.9 9.0 %collective-permute-start = (bf16[1,1,32,768]{3,2,0,1:T(8,128)(2,1)S(1)}, bf16[1,1,32,768]{3,2,0,1:T(8,128)(2,1)S(1)}, u32[]{:S(2)}, u32[]{:S(2)}) collective-permute-start(bf16[1,1,32,768]{3,2,0,1:T(8,128)(2,1)S(1)} %constant_dynamic-slice_fusion.14), channel_id=1, source_target_pairs={{0,2},{2,4},{4,6},{6,8},{8,10},{10,12},{12,14},{14,16},{16,18},{18... | collective-permute-start | bytes 147464 | tf_op jit(solution)/shard_map/ppermute | solution.py:31
  74.9 7.1 %collective-permute-start.1 = (bf16[1,1,32,768]{3,2,0,1:T(8,128)(2,1)S(1)}, bf16[1,1,32,768]{3,2,0,1:T(8,128)(2,1)S(1)}, u32[]{:S(2)}, u32[]{:S(2)}) collective-permute-start(bf16[1,1,32,768]{3,2,0,1:T(8,128)(2,1)S(1)} %get-tuple-element.45), channel_id=1, source_target_pairs={{0,4},{2,6},{4,8},{6,10},{8,12},{10,14},{12,16},{14,18},{16,20},{1... | collective-permute-start | bytes 147464 | tf_op jit(solution)/shard_map/ppermute | solution.py:31
  75.0 9.3 %collective-permute-start.2 = (bf16[1,1,32,768]{3,2,0,1:T(8,128)(2,1)S(1)}, bf16[1,1,32,768]{3,2,0,1:T(8,128)(2,1)S(1)}, u32[]{:S(2)}, u32[]{:S(2)}) collective-permute-start(bf16[1,1,32,768]{3,2,0,1:T(8,128)(2,1)S(1)} %get-tuple-element.44), channel_id=1, source_target_pairs={{0,6},{2,8},{4,10},{6,12},{8,14},{10,16},{12,18},{14,20},{16,22},{... | collective-permute-start | bytes 147464 | tf_op jit(solution)/shard_map/ppermute | solution.py:31
  75.6 10.2 %collective-permute-start.3 = (bf16[1,1,32,768]{3,2,0,1:T(8,128)(2,1)S(1)}, bf16[1,1,32,768]{3,2,0,1:T(8,128)(2,1)S(1)}, u32[]{:S(2)}, u32[]{:S(2)}) collective-permute-start(bf16[1,1,32,768]{3,2,0,1:T(8,128)(2,1)S(1)} %get-tuple-element.43), channel_id=1, source_target_pairs={{0,8},{2,10},{4,12},{6,14},{8,16},{10,18},{12,20},{14,22},{16,24},... | collective-permute-start | bytes 147464 | tf_op jit(solution)/shard_map/ppermute | solution.py:31
  77.1 11.1 %collective-permute-start.4 = (bf16[1,1,32,768]{3,2,0,1:T(8,128)(2,1)S(1)}, bf16[1,1,32,768]{3,2,0,1:T(8,128)(2,1)S(1)}, u32[]{:S(2)}, u32[]{:S(2)}) collective-permute-start(bf16[1,1,32,768]{3,2,0,1:T(8,128)(2,1)S(1)} %get-tuple-element.42), channel_id=1, source_target_pairs={{0,10},{2,12},{4,14},{6,16},{8,18},{10,20},{12,22},{14,24},{16,26}... | collective-permute-start | bytes 147464 | tf_op jit(solution)/shard_map/ppermute | solution.py:31
  79.6 9.3 %collective-permute-start.5 = (bf16[1,1,32,768]{3,2,0,1:T(8,128)(2,1)S(1)}, bf16[1,1,32,768]{3,2,0,1:T(8,128)(2,1)S(1)}, u32[]{:S(2)}, u32[]{:S(2)}) collective-permute-start(bf16[1,1,32,768]{3,2,0,1:T(8,128)(2,1)S(1)} %get-tuple-element.41), channel_id=1, source_target_pairs={{0,12},{2,14},{4,16},{6,18},{8,20},{10,22},{12,24},{14,26},{16,28}... | collective-permute-start | bytes 147464 | tf_op jit(solution)/shard_map/ppermute | solution.py:31
  82.0 9.9 %collective-permute-start.6 = (bf16[1,1,32,768]{3,2,0,1:T(8,128)(2,1)S(1)}, bf16[1,1,32,768]{3,2,0,1:T(8,128)(2,1)S(1)}, u32[]{:S(2)}, u32[]{:S(2)}) collective-permute-start(bf16[1,1,32,768]{3,2,0,1:T(8,128)(2,1)S(1)} %get-tuple-element.40), channel_id=1, source_target_pairs={{0,14},{2,16},{4,18},{6,20},{8,22},{10,24},{12,26},{14,28},{16,30}... | collective-permute-start | bytes 147464 | tf_op jit(solution)/shard_map/ppermute | solution.py:31
  84.3 9.5 %collective-permute-start.7 = (bf16[1,1,32,768]{3,2,0,1:T(8,128)(2,1)S(1)}, bf16[1,1,32,768]{3,2,0,1:T(8,128)(2,1)S(1)}, u32[]{:S(2)}, u32[]{:S(2)}) collective-permute-start(bf16[1,1,32,768]{3,2,0,1:T(8,128)(2,1)S(1)} %get-tuple-element.39), channel_id=1, source_target_pairs={{0,16},{2,18},{4,20},{6,22},{8,24},{10,26},{12,28},{14,30},{16,0},... | collective-permute-start | bytes 147464 | tf_op jit(solution)/shard_map/ppermute | solution.py:31
  85.8 9.1 %collective-permute-start.8 = (bf16[1,1,32,768]{3,2,0,1:T(8,128)(2,1)S(1)}, bf16[1,1,32,768]{3,2,0,1:T(8,128)(2,1)S(1)}, u32[]{:S(2)}, u32[]{:S(2)}) collective-permute-start(bf16[1,1,32,768]{3,2,0,1:T(8,128)(2,1)S(1)} %get-tuple-element.38), channel_id=1, source_target_pairs={{0,18},{2,20},{4,22},{6,24},{8,26},{10,28},{12,30},{14,0},{16,2},{... | collective-permute-start | bytes 147464 | tf_op jit(solution)/shard_map/ppermute | solution.py:31
  88.3 8.5 %collective-permute-start.9 = (bf16[1,1,32,768]{3,2,0,1:T(8,128)(2,1)S(1)}, bf16[1,1,32,768]{3,2,0,1:T(8,128)(2,1)S(1)}, u32[]{:S(2)}, u32[]{:S(2)}) collective-permute-start(bf16[1,1,32,768]{3,2,0,1:T(8,128)(2,1)S(1)} %get-tuple-element.37), channel_id=1, source_target_pairs={{0,20},{2,22},{4,24},{6,26},{8,28},{10,30},{12,0},{14,2},{16,4},{1... | collective-permute-start | bytes 147464 | tf_op jit(solution)/shard_map/ppermute | solution.py:31
  88.9 10.2 %collective-permute-start.10 = (bf16[1,1,32,768]{3,2,0,1:T(8,128)(2,1)S(1)}, bf16[1,1,32,768]{3,2,0,1:T(8,128)(2,1)S(1)}, u32[]{:S(2)}, u32[]{:S(2)}) collective-permute-start(bf16[1,1,32,768]{3,2,0,1:T(8,128)(2,1)S(1)} %get-tuple-element.36), channel_id=1, source_target_pairs={{0,22},{2,24},{4,26},{6,28},{8,30},{10,0},{12,2},{14,4},{16,6},{18... | collective-permute-start | bytes 147464 | tf_op jit(solution)/shard_map/ppermute | solution.py:31
  91.9 7.2 %collective-permute-start.11 = (bf16[1,1,32,768]{3,2,0,1:T(8,128)(2,1)S(1)}, bf16[1,1,32,768]{3,2,0,1:T(8,128)(2,1)S(1)}, u32[]{:S(2)}, u32[]{:S(2)}) collective-permute-start(bf16[1,1,32,768]{3,2,0,1:T(8,128)(2,1)S(1)} %get-tuple-element.35), channel_id=1, source_target_pairs={{0,24},{2,26},{4,28},{6,30},{8,0},{10,2},{12,4},{14,6},{16,8},{18,... | collective-permute-start | bytes 147464 | tf_op jit(solution)/shard_map/ppermute | solution.py:31
  93.8 5.4 collective-permute-start.12
  106.1 21.6 %all-to-all-start.1 = ((bf16[16,32,768]{2,1,0:T(8,128)(2,1)}), bf16[16,32,768]{2,1,0:T(8,128)(2,1)S(1)}, u32[]{:S(2)}, u32[]{:S(2)}) async-start(bf16[16,32,768]{2,1,0:T(8,128)(2,1)} %bitcast.110), calls=%async_computation.2 | async-start | bytes 1572864 | tf_op jit(solution)/shard_map/all_to_all | solution.py:154
  113.3 62.5 %all-gather.7.cloned.1.call-start = ((), (), s32[]{:S(2)}) async-start(), calls=%async_computation.7 | async-start | bytes 2359296 | tf_op jit(solution)/shard_map/all_gather | solution.py:167
  128.5 68.4 %reduce-scatter.7.cloned.1.call-start = ((), (), s32[]{:S(2)}) async-start(), calls=%async_computation.6 | async-start | bytes 2359296 | tf_op jit(solution)/shard_map/reduce_scatter | solution.py:176
  175.4 29.9 %reduce-scatter.9.cloned.1.call-start = ((), (), s32[]{:S(2)}) async-start(), calls=%async_computation.8 | async-start | bytes 2359296 | tf_op jit(solution)/shard_map/reduce_scatter | solution.py:186
  196.9 21.4 %all-to-all-start = ((bf16[16,32,768]{2,1,0:T(8,128)(2,1)}), bf16[16,32,768]{2,1,0:T(8,128)(2,1)S(1)}, u32[]{:S(2)}, u32[]{:S(2)}) async-start(bf16[16,32,768]{2,1,0:T(8,128)(2,1)} %bitcast.112), calls=%async_computation.1 | async-start | bytes 1572864 | tf_op jit(solution)/shard_map/all_to_all | solution.py:192
  218.3 22.5 %all-to-all-start.2 = ((bf16[16,32,768]{2,1,0:T(8,128)(2,1)}), bf16[16,32,768]{2,1,0:T(8,128)(2,1)S(1)}, u32[]{:S(2)}, u32[]{:S(2)}) async-start(bf16[16,32,768]{2,1,0:T(8,128)(2,1)} %bitcast.111), calls=%async_computation.4 | async-start | bytes 1572864 | tf_op jit(solution)/shard_map/all_to_all | solution.py:205
  222.7 135.1 %all-reduce.10.cloned.1.call-start = ((), (), s32[]{:S(2)}) async-start(), calls=%async_computation.9 | async-start | bytes 196608 | tf_op jit(solution)/shard_map/psum | solution.py:268
  235.8 309.2 %all-reduce.12.cloned.1.call-start = ((), (), s32[]{:S(2)}) async-start(), calls=%async_computation.10 | async-start | bytes 9437184 | tf_op jit(solution)/shard_map/psum | solution.py:267
  290.8 12.5 %collective-permute-start.16 = (bf16[3,768]{1,0:T(4,128)(2,1)S(1)}, bf16[3,768]{1,0:T(4,128)(2,1)S(1)}, u32[]{:S(2)}, u32[]{:S(2)}) collective-permute-start(bf16[3,768]{1,0:T(4,128)(2,1)S(1)} %slice.34), channel_id=1, source_target_pairs={{0,1},{2,3},{4,5},{6,7},{8,9},{10,11},{12,13},{14,15},{16,17},{18,... | collective-permute-start | bytes 13832
  (42 other events, 414.5 us)
Sparse Core Ops, SparseCore 0:
  102.0 11.4 all-gather.4
  128.7 8.6 all-gather.6
  175.5 7.8 reduce-scatter.6
  197.0 8.1 reduce-scatter.8
  235.9 121.8 all-reduce.9
  364.0 180.9 all-reduce.11
